TPU v7x, 32 devices: a whole 2x2x4 slice. The times are simulated.
32 devices in a mesh: groups: 2 (over y), sect: 4 (over x, core), hid: 4 (over z).
Axes of the slice: x: 2, y: 2, z: 4, core: 2. Of those that a mesh axis runs over, the one named last changes fastest.
Arguments:
- resid: bfloat16 [1024, 4096], P(('groups', 'sect'), 'hid'), parts along dimension 0, may hold values from -64 to 64
- moe_gain: bfloat16 [4096], replicated, may hold values from 0.25 to 1.75
- routes: int32 [1024, 2], P(('groups', 'sect')), parts along dimension 0, may hold values from 0 to 3, all different within a row; in each aligned block of 128 rows (0 to 127, 128 to 255, ...) at most 128 rows name the same one
- gate_q: int32 [1024, 2], P(('groups', 'sect')), parts along dimension 0, may hold values from 16 to 255
- doc_lengths: int32 [8, 4], P(('groups', 'sect')), parts along dimension 0, may hold values from 1 to 64, 128 in all within a row
- w_gate: bfloat16 [4, 4096, 4096], P('sect', None, 'hid'), may hold values from -0.09375 to 0.09375
- w_up: bfloat16 [4, 4096, 4096], P('sect', None, 'hid'), may hold values from -0.09375 to 0.09375
- w_down: bfloat16 [4, 4096, 4096], P('sect', 'hid'), may hold values from -0.09375 to 0.09375
- attn_gain: bfloat16 [4096], replicated, may hold values from 0.25 to 1.75
- w_q: bfloat16 [4096, 4096], P('sect', 'hid')
- w_k: bfloat16 [4096, 1024], P('sect', 'hid')
- w_v: bfloat16 [4096, 1024], P('sect', 'hid'), may hold values from -0.09375 to 0.09375
Outputs:
- new_resid: bfloat16 [1024, 4096], P(('groups', 'sect'), 'hid'), parts along dimension 0
- context: bfloat16 [1024, 4096], P(('groups', 'sect'), 'hid'), parts along dimension 0
There are 2 independent parts, one for each index of `groups`. A program takes and returns all parts, laid end to end along the dimension named above; an argument that names none is the same for every part. Nothing has to cross between parts.
Inputs may be any that keep to these rules, and one draw needn't show every extreme that they name: `routes`: within the rows of one index of sect (aligned blocks of 128 rows) no expert is named by more than 128 rows. `doc_lengths`: each row sums to 128.
All inputs are finite; a program needn't handle non-finite values.
Results may differ from a plain program's by a relative error of at most 0.012.
The roundings to bfloat16 on the way count: a program that leaves them out, or rounds other values in their place, can miss the bound.
Values may be sent and summed in bfloat16 or wider, within the bound.
No kernel may reach another device: no remote copies, remote signals or barrier semaphores. Data moves between devices by JAX's collectives and lax.ppermute only.
A program may use at most 128 MiB of HBM per device.

v0:
```python
import math
import jax
import jax.numpy as jnp
from jax import lax
from jax.sharding import PartitionSpec as P

H = 32
KVH = 8
HD = 128


def layer_norm(values, gain):
    center = values - jnp.mean(values, axis=1, keepdims=True)
    spread = jnp.mean(center * center, axis=1, keepdims=True)
    return (center * lax.rsqrt(spread + 1e-05) * gain.astype(jnp.float32)).astype(jnp.bfloat16)


def slot_targets(route_rows, experts, capacity):
    flat = route_rows.reshape(-1)
    onehot = (flat[:, None] == jnp.arange(experts, dtype=jnp.int32)[None, :]).astype(jnp.int32)
    before = jnp.cumsum(onehot, axis=0, dtype=jnp.int32) - onehot
    return flat * capacity + jnp.sum(before * onehot, axis=1, dtype=jnp.int32)


def source_rows(targets, experts, capacity):
    count = targets.shape[0]
    filler = jnp.full((experts * capacity,), count, jnp.int32)
    return filler.at[targets].set(jnp.arange(count, dtype=jnp.int32)) // 2


def rotate(values, position, head):
    count = values.shape[0]
    split_heads = values.reshape(count, -1, head)
    half = head // 2
    freqs = jnp.exp(jnp.arange(half, dtype=jnp.float32) * (-2.0 * math.log(10000.0) / head))
    angles = position[:, None, None] * freqs[None, None, :]
    cosine = jnp.cos(angles)
    sine = jnp.sin(angles)
    first = split_heads[:, :, :half]
    second = split_heads[:, :, half:]
    turned = jnp.concatenate(
        [first * cosine - second * sine, second * cosine + first * sine], axis=2
    )
    return turned.reshape(count, -1)


def attend(query, keys, vals, lengths, head, group):
    count = query.shape[0]
    kv_heads = keys.shape[1] // head
    ends = jnp.cumsum(lengths, dtype=jnp.int32)
    places = jnp.arange(count, dtype=jnp.int32)
    after = (places[:, None] >= ends[None, :]).astype(jnp.int32)
    doc_ids = jnp.sum(after, axis=1, dtype=jnp.int32)
    starts = jnp.sum(after * lengths[None, :], axis=1, dtype=jnp.int32)
    position = (places - starts).astype(jnp.float32)
    rotated_q = (
        rotate(query, position, head).astype(jnp.bfloat16).reshape(count, kv_heads, group, head)
    )
    rotated_k = rotate(keys, position, head).astype(jnp.bfloat16).reshape(count, kv_heads, head)
    value_heads = vals.reshape(count, kv_heads, head)
    allowed = (doc_ids[:, None] == doc_ids[None, :]) & (places[None, :] <= places[:, None])
    scores = jnp.einsum(
        "tkgd,skd->kgts", rotated_q, rotated_k, preferred_element_type=jnp.float32
    ) * (1.0 / math.sqrt(head))
    scores = jnp.where(allowed[None, None], scores, -jnp.inf)
    highest = jnp.max(scores, axis=3, keepdims=True)
    weights = jnp.exp(scores - highest)
    probs = (weights / jnp.sum(weights, axis=3, keepdims=True)).astype(jnp.bfloat16)
    mixed = jnp.einsum("kgts,skd->tkgd", probs, value_heads, preferred_element_type=jnp.float32)
    return mixed.astype(jnp.bfloat16).reshape(count, -1)


def on_device(
    resid, moe_gain, routes, gate_q, doc_lengths, w_gate, w_up, w_down, attn_gain, w_q, w_k, w_v
):
    sections = lax.axis_size("sect")
    slices = lax.axis_size("hid")
    tokens_here, local_width = resid.shape
    width = local_width * slices
    capacity = 4 * tokens_here // sections
    entry = lax.all_gather(resid, "hid", axis=1, tiled=True)
    normed = layer_norm(entry.astype(jnp.float32), moe_gain)
    targets = slot_targets(routes, sections, capacity)
    sources = source_rows(targets, sections, capacity)
    padded = jnp.concatenate([normed, jnp.zeros((1, width), jnp.bfloat16)], axis=0)
    gate_w = w_gate[0]
    up_w = w_up[0]
    down_w = w_down[0]
    outgoing = padded[sources].reshape(sections, capacity, width)
    arrived = lax.all_to_all(outgoing, "sect", split_axis=0, concat_axis=0, tiled=True).reshape(
        sections * capacity, width
    )
    gate = jnp.dot(arrived, gate_w, preferred_element_type=jnp.float32)
    up = jnp.dot(arrived, up_w, preferred_element_type=jnp.float32)
    hidden = (jax.nn.silu(gate) * up).astype(jnp.bfloat16)
    weights = gate_q.reshape(-1).astype(jnp.float32) / 256.0
    own_resid = resid.astype(jnp.float32)
    outputs = jnp.dot(hidden, down_w, preferred_element_type=jnp.float32)
    mine = lax.psum_scatter(outputs, "hid", scatter_dimension=1, tiled=True)
    returned = lax.all_to_all(
        mine.reshape(sections, capacity, local_width),
        "sect",
        split_axis=0,
        concat_axis=0,
        tiled=True,
    )
    picked = returned.reshape(sections * capacity, local_width)[targets]
    mixture = jnp.sum((picked * weights[:, None]).reshape(tokens_here, 2, local_width), axis=1)
    new_local = (own_resid + mixture).astype(jnp.bfloat16)
    full_rows = lax.all_gather(new_local, "hid", axis=1, tiled=True)
    normed_next = layer_norm(full_rows.astype(jnp.float32), attn_gain)
    query = jnp.dot(
        normed_next,
        lax.all_gather(w_q, "sect", axis=0, tiled=True),
        preferred_element_type=jnp.float32,
    )
    keys = jnp.dot(
        normed_next,
        lax.all_gather(w_k, "sect", axis=0, tiled=True),
        preferred_element_type=jnp.float32,
    )
    vals = jnp.dot(
        normed_next,
        lax.all_gather(w_v, "sect", axis=0, tiled=True),
        preferred_element_type=jnp.float32,
    )
    context = attend(query, keys, vals.astype(jnp.bfloat16), doc_lengths[0], HD, H // KVH)
    return (new_local, context)


def solution(mesh):
    in_specs = (
        P(("groups", "sect"), "hid"),
        P(),
        P(("groups", "sect"), None),
        P(("groups", "sect"), None),
        P(("groups", "sect"), None),
        P("sect", None, "hid"),
        P("sect", None, "hid"),
        P("sect", "hid", None),
        P(),
        P("sect", "hid"),
        P("sect", "hid"),
        P("sect", "hid"),
    )
    out_specs = (P(("groups", "sect"), "hid"), P(("groups", "sect"), "hid"))
    return jax.shard_map(
        on_device, mesh=mesh, in_specs=in_specs, out_specs=out_specs, check_vma=False
    )
```

profile of v0, /device:TPU:0, one launch (start us, length us, event | category | flops | bytes accessed | tf_op | source)
XLA Modules:
  0.0 450.2 jit_solution(11100007344031387848)
XLA Ops:
  9.7 1.2 reduce-window.18
  12.3 1.4 scatter_custom_fusion
  13.7 26.5 %all-gather.6.cloned.1.call-done = bf16[128,4096]{1,0:T(8,128)(2,1)} async-done(((bf16[128,1024]{1,0:T(8,128)(2,1)}), bf16[128,4096]{1,0:T(8,128)(2,1)}) %all-gather.6.cloned.1.call-update) | async-done | bytes 1048592 | tf_op jit(solution)/shard_map/all_gather | solution.py:81
  40.2 1.5 convert_reduce_fusion.1
  41.8 1.7 fusion.14
  44.0 4.4 gather_fusion
  48.3 51.9 %all_to_all.10 = bf16[4,128,4096]{2,1,0:T(8,128)(2,1)S(1)} all-to-all(bf16[4,128,4096]{2,1,0:T(8,128)(2,1)} %bitcast.87), channel_id=1, replica_groups=mesh['groups'=2,'sect'=4,'hid'=4] {'sect'}, dimensions={0} | all-to-all | bytes 8388608 | tf_op jit(solution)/shard_map/all_to_all | solution.py:90
  100.2 2.0 copy-done.1
  102.2 6.9 %fusion.5 = f32[512,1024]{1,0:T(8,128)S(1)} fusion(bf16[512,4096]{1,0:T(8,128)(2,1)S(1)} %bitcast.89, bf16[1,4096,1024]{2,1,0:T(8,128)(2,1)} %param.17), kind=kOutput, calls=%fused_computation.8 | convolution fusion | flops 4294967296 | bytes 14680064 | tf_op jit(solution)/shard_map/dot_general | solution.py:93
  109.1 19.1 %fusion.1 = f32[512,4096]{1,0:T(8,128)} fusion(bf16[1,1024,4096]{2,1,0:T(8,128)(2,1)} %param.19, f32[512,1024]{1,0:T(8,128)S(1)} %fusion.5, bf16[512,4096]{1,0:T(8,128)(2,1)} %bitcast.90, bf16[1,4096,1024]{2,1,0:T(8,128)(2,1)} %param.18), kind=kOutput, calls=%fused_computation.4 | convolution fusion | flops 8593080320 | bytes 31457280 | tf_op jit(solution)/shard_map/dot_general | solution.py:98
  128.2 143.2 %reduce-scatter.2.cloned.1.call-done = f32[512,1024]{1,0:T(8,128)} async-done(((f32[512,4096]{1,0:T(8,128)}), f32[512,1024]{1,0:T(8,128)}) %reduce-scatter.2.cloned.1.call-update) | async-done | bytes 2097168 | tf_op jit(solution)/shard_map/reduce_scatter | solution.py:99
  271.4 3.7 all-to-all-start.1
  275.5 25.3 %all-to-all-done.1 = f32[4,128,1024]{2,1,0:T(8,128)S(1)} async-done(((f32[4,128,1024]{2,1,0:T(8,128)}), f32[4,128,1024]{2,1,0:T(8,128)S(1)}, u32[]{:S(2)}, u32[]{:S(2)}) %all-to-all-start.1) | async-done | bytes 2097184 | tf_op jit(solution)/shard_map/all_to_all | solution.py:100
  300.8 1.1 gather_fusion.1
  302.6 1.3 multiply_reduce_fusion
  307.2 25.4 %all-gather.8.cloned.1.call-done = bf16[128,4096]{1,0:T(8,128)(2,1)} async-done(((bf16[128,1024]{1,0:T(8,128)(2,1)}), bf16[128,4096]{1,0:T(8,128)(2,1)}) %all-gather.8.cloned.1.call-update) | async-done | bytes 1048592 | tf_op jit(solution)/shard_map/all_gather | solution.py:110
  332.6 1.5 convert_reduce_fusion
  334.2 1.7 fusion.11
  335.9 20.3 %all-gather.12.cloned.1.call-done = bf16[4096,256]{1,0:T(8,128)(2,1)} async-done(((bf16[1024,256]{1,0:T(8,128)(2,1)}), bf16[4096,256]{1,0:T(8,128)(2,1)}) %all-gather.12.cloned.1.call-update) | async-done | bytes 2097168 | tf_op jit(solution)/shard_map/all_gather | solution.py:119
  356.2 2.1 fusion.40
  358.4 57.5 %all-gather.14.cloned.1.call-done = bf16[4096,1024]{1,0:T(8,128)(2,1)} async-done(((bf16[1024,1024]{1,0:T(8,128)(2,1)}), bf16[4096,1024]{1,0:T(8,128)(2,1)}) %all-gather.14.cloned.1.call-update) | async-done | bytes 8388624 | tf_op jit(solution)/shard_map/all_gather | solution.py:114
  415.9 4.7 %convolution_bitcast_fusion = f32[16,8,8,128]{3,1,2,0:T(8,128)S(1)} fusion(bf16[4096,1024]{1,0:T(8,128)(2,1)} %all-gather.14.cloned.1.call-done, bf16[128,4096]{1,0:T(8,128)(2,1)S(1)} %copy-done.2, f32[4096]{0:T(1024)S(1)} %convert_element_type.80, f32[128]{0:T(128)S(1)} %add_rsqrt_fusion, f32[128]{0:T(128)S(1)} %broadcast_multiply_fusion.1), kind=kOutput, calls=%fused_computation.27 | convolution fusion | flops 1076363264 | bytes 9978880 | tf_op jit(solution)/shard_map/dot_general | solution.py:112
  422.1 17.9 %all-gather.10.cloned.1.call-done = bf16[4096,256]{1,0:T(8,128)(2,1)} async-done(((bf16[1024,256]{1,0:T(8,128)(2,1)}), bf16[4096,256]{1,0:T(8,128)(2,1)}) %all-gather.10.cloned.1.call-update) | async-done | bytes 2097168 | tf_op jit(solution)/shard_map/all_gather | solution.py:124
  439.9 2.1 convolution_convert_fusion.1
  (74 shorter events, 11.4 us)
Async XLA Ops:
  7.2 33.1 %all-gather.6.cloned.1.call-start = ((), (), s32[]{:S(2)}) async-start(), calls=%async_computation.3 | async-start | bytes 1310720 | tf_op jit(solution)/shard_map/all_gather | solution.py:81
  7.9 263.5 %reduce-scatter.2.cloned.1.call-start = ((), (), s32[]{:S(2)}) async-start(), calls=%async_computation.4 | async-start | bytes 10485760 | tf_op jit(solution)/shard_map/reduce_scatter | solution.py:99
  40.2 3.2 copy-start
  100.2 2.0 copy-start.1
  271.4 4.0 copy-start.5
  271.4 29.4 %all-to-all-start.1 = ((f32[4,128,1024]{2,1,0:T(8,128)}), f32[4,128,1024]{2,1,0:T(8,128)S(1)}, u32[]{:S(2)}, u32[]{:S(2)}) async-start(f32[4,128,1024]{2,1,0:T(8,128)} %bitcast.91), calls=%async_computation.2 | async-start | bytes 4194304 | tf_op jit(solution)/shard_map/all_to_all | solution.py:100
  275.2 57.5 %all-gather.8.cloned.1.call-start = ((), (), s32[]{:S(2)}) async-start(), calls=%async_computation.5 | async-start | bytes 1310720 | tf_op jit(solution)/shard_map/all_gather | solution.py:110
  301.9 2.0 copy-start.3
  303.9 2.6 copy-start.4
  303.9 2.6 copy-start.6
  304.7 51.4 %all-gather.12.cloned.1.call-start = ((), (), s32[]{:S(2)}) async-start(), calls=%async_computation.7 | async-start | bytes 2621440 | tf_op jit(solution)/shard_map/all_gather | solution.py:119
  305.3 110.6 %all-gather.14.cloned.1.call-start = ((), (), s32[]{:S(2)}) async-start(), calls=%async_computation.8 | async-start | bytes 10485760 | tf_op jit(solution)/shard_map/all_gather | solution.py:114
  305.9 134.0 %all-gather.10.cloned.1.call-start = ((), (), s32[]{:S(2)}) async-start(), calls=%async_computation.6 | async-start | bytes 2621440 | tf_op jit(solution)/shard_map/all_gather | solution.py:124
  332.6 23.5 %copy-start.2 = (bf16[128,4096]{1,0:T(8,128)(2,1)S(1)}, bf16[128,4096]{1,0:T(8,128)(2,1)}, u32[]{:S(2)}) copy-start(bf16[128,4096]{1,0:T(8,128)(2,1)} %all-gather.8.cloned.1.call-done) | copy-start | bytes 3145732
Sparse Core Ops, SparseCore 0:
  9.6 30.6 all-gather.5
  128.3 143.0 reduce-scatter.1
  304.9 27.7 all-gather.7
  334.1 22.0 all-gather.11
  357.6 58.2 all-gather.13
  417.3 22.5 all-gather.9
where the time goes:
time: 451 us; the launch traced here: 450 us
  waiting for transfers between devices  318 us (71%)
  blocking collectives  51.9 us (12%)
  matrix products  35.8 us (8%)
  between operations  14.4 us (3%)
  other arithmetic  12.8 us (3%)
  local copies, waits for them, and re-layouts  12.6 us (3%)
    reduce_scatter x1, waiting for transfers between devices, on_device(): mine = lax.psum_scatter(outputs, 'hid', scatter_dimension=1, tiled=True)  143 us
    all_gather x1, waiting for transfers between devices, on_device(): lax.all_gather(w_q, 'sect', axis=0, tiled=True)  57.5 us
    all_to_all x1, blocking collectives, on_device(): lax.all_to_all(outgoing, 'sect', split_axis=0, concat_axis=0, tiled=True)  51.9 us
    all_gather x1, waiting for transfers between devices, on_device(): entry = lax.all_gather(resid, 'hid', axis=1, tiled=True)  26.5 us
    all_gather x1, waiting for transfers between devices, on_device(): full_rows = lax.all_gather(new_local, 'hid', axis=1, tiled=True)  25.4 us
    all_to_all x1, waiting for transfers between devices, on_device(): lax.all_to_all(mine.reshape(sections, capacity, local_width), 'sect', spl...  25.3 us
    all_gather x1, waiting for transfers between devices, on_device(): lax.all_gather(w_k, 'sect', axis=0, tiled=True)  20.3 us
    dot_general x1, matrix products, on_device(): outputs = jnp.dot(hidden, down_w, preferred_element_type=jnp.float32)  19.1 us
  transfers between devices with their start and end apart: 7, of which 7 were waited for; matrix products, arithmetic and copies ran while one was open for 4% of the time, Pallas kernels for 0%

commit v1 on v0

--- a/solution.py
+++ b/solution.py
@@ -7,6 +7,19 @@
 H = 32
 KVH = 8
 HD = 128
+
+
+def ring_gather(x, axis, dim):
+    ways = lax.axis_size(axis)
+    up = [(d, (d + 1) % ways) for d in range(ways)]
+    down = [(d, (d - 1) % ways) for d in range(ways)]
+    earlier, later = ([x], [x])
+    for _ in range(ways // 2):
+        earlier.append(lax.ppermute(earlier[-1], axis, up))
+    for _ in range((ways - 1) // 2):
+        later.append(lax.ppermute(later[-1], axis, down))
+    line = jnp.concatenate([*earlier[::-1], *later[1:]], axis=dim)
+    return jnp.roll(line, (lax.axis_index(axis) - ways // 2) * x.shape[dim], axis=dim)
 
 
 def layer_norm(values, gain):
@@ -107,7 +120,7 @@
     picked = returned.reshape(sections * capacity, local_width)[targets]
     mixture = jnp.sum((picked * weights[:, None]).reshape(tokens_here, 2, local_width), axis=1)
     new_local = (own_resid + mixture).astype(jnp.bfloat16)
-    full_rows = lax.all_gather(new_local, "hid", axis=1, tiled=True)
+    full_rows = ring_gather(new_local, "hid", 1)
     normed_next = layer_norm(full_rows.astype(jnp.float32), attn_gain)
     query = jnp.dot(
         normed_next,

time: 451 us -> 360 us (0.80)
  waiting for transfers between devices: 318 us -> 224 us
  starting transfers between devices: 4.15 us -> 9.19 us
    all_gather x1, waiting for transfers between devices: 57.5 us -> 0.03 us  [on_device(): lax.all_gather(w_q, 'sect', axis=0, tiled=True)]
    all_gather x1 -> x0, waiting for transfers between devices: 25.4 us -> none  [on_device(): full_rows = lax.all_gather(new_local, 'hid', axis=1, tiled=True)]
    all_gather x1, waiting for transfers between devices: 20.3 us -> 0.03 us  [on_device(): lax.all_gather(w_k, 'sect', axis=0, tiled=True)]
    all_gather x1, waiting for transfers between devices: 17.9 us -> 0.03 us  [on_device(): lax.all_gather(w_v, 'sect', axis=0, tiled=True)]
    ppermute x0 -> x3, waiting for transfers between devices: none -> 17.1 us  [the longest x2 15.2 us: ring_gather(): earlier.append(lax.ppermute(earlier[-1], axis, up))]
    all_to_all x1, waiting for transfers between devices: 25.3 us -> 35.9 us  [on_device(): lax.all_to_all(mine.reshape(sections, capacity, local_width), 'sect', spl...]
    ppermute x0 -> x3, starting transfers between devices: none -> 5.07 us  [the longest x1 3.84 us: ring_gather(): later.append(lax.ppermute(later[-1], axis, down))]
  transfers between devices with their start and end apart: 7 -> 9, of which waited for: 7 -> 6; matrix products, arithmetic and copies ran while one was open for 4% -> 5% of each run, Pallas kernels for 0% -> 0%
where the time goes in v1:
time: 360 us; the launch traced here: 359 us
  waiting for transfers between devices  224 us (62%)
  blocking collectives  51.9 us (14%)
  matrix products  35.8 us (10%)
  between operations  16.1 us (4%)
  local copies, waits for them, and re-layouts  12.7 us (4%)
  other arithmetic  9.59 us (3%)
  starting transfers between devices  9.19 us (3%)
    reduce_scatter x1, waiting for transfers between devices, on_device(): mine = lax.psum_scatter(outputs, 'hid', scatter_dimension=1, tiled=True)  142 us
    all_to_all x1, blocking collectives, on_device(): lax.all_to_all(outgoing, 'sect', split_axis=0, concat_axis=0, tiled=True)  51.9 us
    all_to_all x1, waiting for transfers between devices, on_device(): lax.all_to_all(mine.reshape(sections, capacity, local_width), 'sect', spl...  35.9 us
    all_gather x1, waiting for transfers between devices, on_device(): entry = lax.all_gather(resid, 'hid', axis=1, tiled=True)  26.5 us
    dot_general x1, matrix products, on_device(): outputs = jnp.dot(hidden, down_w, preferred_element_type=jnp.float32)  19.1 us
    ppermute x2, waiting for transfers between devices, ring_gather(): earlier.append(lax.ppermute(earlier[-1], axis, up))  15.2 us
  transfers between devices with their start and end apart: 9, of which 6 were waited for; matrix products, arithmetic and copies ran while one was open for 5% of the time, Pallas kernels for 0%

profile of v1, /device:TPU:0, one launch (start us, length us, event | category | flops | bytes accessed | tf_op | source)
XLA Modules:
  0.0 359.0 jit_solution(14182774999484378171)
XLA Ops:
  10.6 1.2 reduce-window.18
  13.1 1.4 scatter_custom_fusion
  14.6 26.5 %all-gather.5.cloned.1.call-done = bf16[128,4096]{1,0:T(8,128)(2,1)} async-done(((bf16[128,1024]{1,0:T(8,128)(2,1)}), bf16[128,4096]{1,0:T(8,128)(2,1)}) %all-gather.5.cloned.1.call-update) | async-done | bytes 1048592 | tf_op jit(solution)/shard_map/all_gather | solution.py:94
  41.1 1.5 convert_reduce_fusion.1
  42.6 1.7 fusion.14
  44.8 4.4 %gather_fusion = bf16[512,4096]{1,0:T(8,128)(2,1)} fusion(bf16[129,4096]{1,0:T(8,128)(2,1)S(1)} %concatenate.17, s32[1024]{0:T(1024)S(1)} %pad_clamp_fusion.1), kind=kCustom, calls=%fused_computation | custom fusion | bytes 8390656 | tf_op jit(solution)/shard_map/gather | solution.py:102
  49.2 51.9 %all_to_all.10 = bf16[4,128,4096]{2,1,0:T(8,128)(2,1)S(1)} all-to-all(bf16[4,128,4096]{2,1,0:T(8,128)(2,1)} %bitcast.87), channel_id=1, replica_groups=mesh['groups'=2,'sect'=4,'hid'=4] {'sect'}, dimensions={0} | all-to-all | bytes 8388608 | tf_op jit(solution)/shard_map/all_to_all | solution.py:103
  101.1 1.9 copy-done.1
  103.0 6.9 %fusion.5 = f32[512,1024]{1,0:T(8,128)S(1)} fusion(bf16[512,4096]{1,0:T(8,128)(2,1)S(1)} %bitcast.89, bf16[1,4096,1024]{2,1,0:T(8,128)(2,1)} %param.17), kind=kOutput, calls=%fused_computation.8 | convolution fusion | flops 4294967296 | bytes 14680064 | tf_op jit(solution)/shard_map/dot_general | solution.py:106
  109.9 19.1 %fusion.1 = f32[512,4096]{1,0:T(8,128)} fusion(bf16[1,1024,4096]{2,1,0:T(8,128)(2,1)} %param.19, f32[512,1024]{1,0:T(8,128)S(1)} %fusion.5, bf16[512,4096]{1,0:T(8,128)(2,1)} %bitcast.90, bf16[1,4096,1024]{2,1,0:T(8,128)(2,1)} %param.18), kind=kOutput, calls=%fused_computation.4 | convolution fusion | flops 8593080320 | bytes 31457280 | tf_op jit(solution)/shard_map/dot_general | solution.py:111
  130.1 142.1 %reduce-scatter.2.cloned.1.call-done = f32[512,1024]{1,0:T(8,128)} async-done(((f32[512,4096]{1,0:T(8,128)}), f32[512,1024]{1,0:T(8,128)}) %reduce-scatter.2.cloned.1.call-update) | async-done | bytes 2097168 | tf_op jit(solution)/shard_map/reduce_scatter | solution.py:112
  272.2 3.7 %all-to-all-start.1 = ((f32[4,128,1024]{2,1,0:T(8,128)}), f32[4,128,1024]{2,1,0:T(8,128)S(1)}, u32[]{:S(2)}, u32[]{:S(2)}) async-start(f32[4,128,1024]{2,1,0:T(8,128)} %bitcast.91), calls=%async_computation.2 | async-start | bytes 4194304 | tf_op jit(solution)/shard_map/all_to_all | solution.py:113
  276.9 35.9 %all-to-all-done.1 = f32[4,128,1024]{2,1,0:T(8,128)S(1)} async-done(((f32[4,128,1024]{2,1,0:T(8,128)}), f32[4,128,1024]{2,1,0:T(8,128)S(1)}, u32[]{:S(2)}, u32[]{:S(2)}) %all-to-all-start.1) | async-done | bytes 2097184 | tf_op jit(solution)/shard_map/all_to_all | solution.py:113
  312.8 1.1 gather_fusion.1
  314.6 1.3 multiply_reduce_fusion
  316.0 1.2 collective-permute-start
  317.3 8.4 %collective-permute-done = bf16[128,1024]{1,0:T(8,128)(2,1)S(1)} collective-permute-done((bf16[128,1024]{1,0:T(8,128)(2,1)S(1)}, bf16[128,1024]{1,0:T(8,128)(2,1)S(1)}, u32[]{:S(2)}, u32[]{:S(2)}) %collective-permute-start) | collective-permute-done | bytes 262176 | tf_op jit(solution)/shard_map/ppermute | solution.py:18
  326.1 3.8 %collective-permute-start.2 = (bf16[128,1024]{1,0:T(8,128)(2,1)S(1)}, bf16[128,1024]{1,0:T(8,128)(2,1)S(1)}, u32[]{:S(2)}, u32[]{:S(2)}) collective-permute-start(bf16[128,1024]{1,0:T(8,128)(2,1)S(1)} %add_convert_fusion.1), channel_id=1, source_target_pairs={{0,3},{1,0},{2,1},{3,2},{4,7},{5,4},{6,5},{7,6},{8,11},{9,8},{10,9... | collective-permute-start | bytes 786440 | tf_op jit(solution)/shard_map/ppermute | solution.py:20
  329.9 6.8 %collective-permute-done.1 = bf16[128,1024]{1,0:T(8,128)(2,1)S(1)} collective-permute-done((bf16[128,1024]{1,0:T(8,128)(2,1)S(1)}, bf16[128,1024]{1,0:T(8,128)(2,1)S(1)}, u32[]{:S(2)}, u32[]{:S(2)}) %collective-permute-start.1) | collective-permute-done | bytes 262176 | tf_op jit(solution)/shard_map/ppermute | solution.py:18
  336.8 1.9 collective-permute-done.2
  339.6 2.1 fusion.40
  341.8 4.7 %convolution_bitcast_fusion = f32[16,8,8,128]{3,1,2,0:T(8,128)S(1)} fusion(bf16[4096,1024]{1,0:T(8,128)(2,1)} %all-gather.11.cloned.1.call-done, f32[4096]{0:T(1024)S(1)} %convert_element_type.80, f32[128]{0:T(128)S(1)} %add_rsqrt_fusion, f32[128]{0:T(128)S(1)} %broadcast_multiply_fusion.1, bf16[128,8192]{1,0:T(8,128)(2,1)S(1)} %constant_dynamic-update-slice_fusion, ...), kind=kOutput, calls=%fused_computation.27 | convolution fusion | flops 1076363264 | bytes 9978884 | tf_op jit(solution)/shard_map/dot_general | solution.py:125
  348.0 2.1 convolution_convert_fusion.1
  350.6 0.9 copy.46
  (85 shorter events, 10.5 us)
Async XLA Ops:
  8.0 33.1 %all-gather.5.cloned.1.call-start = ((), (), s32[]{:S(2)}) async-start(), calls=%async_computation.3 | async-start | bytes 1310720 | tf_op jit(solution)/shard_map/all_gather | solution.py:94
  8.7 263.5 %reduce-scatter.2.cloned.1.call-start = ((), (), s32[]{:S(2)}) async-start(), calls=%async_computation.4 | async-start | bytes 10485760 | tf_op jit(solution)/shard_map/reduce_scatter | solution.py:112
  41.1 3.2 copy-start
  101.1 1.9 copy-start.1
  129.0 210.6 %all-gather.9.cloned.1.call-start = ((), (), s32[]{:S(2)}) async-start(), calls=%async_computation.6 | async-start | bytes 2621440 | tf_op jit(solution)/shard_map/all_gather | solution.py:132
  129.5 212.2 %all-gather.11.cloned.1.call-start = ((), (), s32[]{:S(2)}) async-start(), calls=%async_computation.7 | async-start | bytes 10485760 | tf_op jit(solution)/shard_map/all_gather | solution.py:127
  272.2 4.3 %copy-start.5 = (s32[128,2]{0,1:T(2,128)S(1)}, s32[128,2]{0,1:T(2,128)}, u32[]{:S(2)}) copy-start(s32[128,2]{0,1:T(2,128)} %param.15) | copy-start | bytes 3076
  272.2 4.5 %copy-start.6 = (s32[1,4]{1,0:T(1,128)S(1)}, s32[1,4]{1,0:T(1,128)}, u32[]{:S(2)}) copy-start(s32[1,4]{1,0:T(1,128)} %param.16) | copy-start | bytes 52
  272.2 40.6 %all-to-all-start.1 = ((f32[4,128,1024]{2,1,0:T(8,128)}), f32[4,128,1024]{2,1,0:T(8,128)S(1)}, u32[]{:S(2)}, u32[]{:S(2)}) async-start(f32[4,128,1024]{2,1,0:T(8,128)} %bitcast.91), calls=%async_computation.2 | async-start | bytes 4194304 | tf_op jit(solution)/shard_map/all_to_all | solution.py:113
  275.9 72.1 %all-gather.7.cloned.1.call-start = ((), (), s32[]{:S(2)}) async-start(), calls=%async_computation.5 | async-start | bytes 2621440 | tf_op jit(solution)/shard_map/all_gather | solution.py:137
  313.9 2.0 copy-start.3
  313.9 11.8 %copy-start.4 = (bf16[4096]{0:T(1024)(128)(2,1)S(1)}, bf16[4096]{0:T(1024)(128)(2,1)}, u32[]{:S(2)}) copy-start(bf16[4096]{0:T(1024)(128)(2,1)} %param.20) | copy-start | bytes 24580
  316.0 22.8 %copy-start.2 = (bf16[128,1024]{1,0:T(8,128)(2,1)}, bf16[128,1024]{1,0:T(8,128)(2,1)S(1)}, u32[]{:S(2)}) copy-start(bf16[128,1024]{1,0:T(8,128)(2,1)S(1)} %add_convert_fusion.1) | copy-start | bytes 786436
  316.0 9.7 %collective-permute-start = (bf16[128,1024]{1,0:T(8,128)(2,1)S(1)}, bf16[128,1024]{1,0:T(8,128)(2,1)S(1)}, u32[]{:S(2)}, u32[]{:S(2)}) collective-permute-start(bf16[128,1024]{1,0:T(8,128)(2,1)S(1)} %add_convert_fusion.1), channel_id=1, source_target_pairs={{0,1},{1,2},{2,3},{3,0},{4,5},{5,6},{6,7},{7,4},{8,9},{9,10},{10,1... | collective-permute-start | bytes 786440 | tf_op jit(solution)/shard_map/ppermute | solution.py:18
  325.7 11.0 %collective-permute-start.1 = (bf16[128,1024]{1,0:T(8,128)(2,1)S(1)}, bf16[128,1024]{1,0:T(8,128)(2,1)S(1)}, u32[]{:S(2)}, u32[]{:S(2)}) collective-permute-start(bf16[128,1024]{1,0:T(8,128)(2,1)S(1)} %collective-permute-done), channel_id=1, source_target_pairs={{0,1},{1,2},{2,3},{3,0},{4,5},{5,6},{6,7},{7,4},{8,9},{9,10},{10,1... | collective-permute-start | bytes 786440 | tf_op jit(solution)/shard_map/ppermute | solution.py:18
  326.1 12.6 %collective-permute-start.2 = (bf16[128,1024]{1,0:T(8,128)(2,1)S(1)}, bf16[128,1024]{1,0:T(8,128)(2,1)S(1)}, u32[]{:S(2)}, u32[]{:S(2)}) collective-permute-start(bf16[128,1024]{1,0:T(8,128)(2,1)S(1)} %add_convert_fusion.1), channel_id=1, source_target_pairs={{0,3},{1,0},{2,1},{3,2},{4,7},{5,4},{6,5},{7,6},{8,11},{9,8},{10,9... | collective-permute-start | bytes 786440 | tf_op jit(solution)/shard_map/ppermute | solution.py:20
Sparse Core Ops, SparseCore 0:
  10.4 30.6 all-gather.4
  129.1 143.0 reduce-scatter.1
Sparse Core Ops, SparseCore 1:
  131.0 21.0 all-gather.8
  153.5 58.1 all-gather.10
  278.0 35.0 all-gather.6
